TPU v7x, 256 devices: a whole 4x4x8 slice. The times are simulated.
256 devices in a mesh: dp: 4 (over x), vocab: 64 (over z, y, core).
Axes of the slice: x: 4, y: 4, z: 8, core: 2. Of those that a mesh axis runs over, the one named last changes fastest.
Arguments:
- hidden_t: bfloat16 [8192, 768], P(('dp', 'vocab')), may hold values from -6 to 6
- head: bfloat16 [8192, 81920], P('dp', 'vocab'), may hold values from -0.2 to 0.2
- teacher: bfloat16 [768, 81920], P('dp', 'vocab'), may hold values from -16 to 960
- labels: int32 [768], P('dp'), may hold values from 0 to 81919
- temps: float32 [4], replicated, may hold values from 1 to 4
- mix: float32 [2], replicated, may hold values from 0.3 to 1
Outputs:
- hidden_grad: float32 [8192, 768], P(('dp', 'vocab'))
- head_grad: bfloat16 [8192, 81920], P('dp', 'vocab')
All inputs are finite; a program needn't handle non-finite values.
Results may differ from a plain program's by a relative error of at most 0.012.
Values may be sent and summed in bfloat16 or wider, within the bound.
A program may use at most 128 MiB of HBM per device.

v0:
```python
import jax
import jax.numpy as jnp
from jax import lax
from jax.sharding import PartitionSpec as P


def shards(hidden_t, head, teacher, labels, temps, mix):
    h_block = lax.all_gather(hidden_t, "vocab", axis=0, tiled=True)
    block_width = head.shape[1]
    logits = lax.psum_scatter(
        lax.dot_general(
            h_block, head, (((0,), (0,)), ((), ())), preferred_element_type=jnp.float32
        ),
        "dp",
        scatter_dimension=0,
        tiled=True,
    )
    target = teacher.astype(jnp.float32)
    inverse = 1.0 / temps
    student = jnp.concatenate([logits[None], logits[None] * inverse[:, None, None]], axis=0)
    teacher_scaled = target[None] * inverse[:, None, None]
    stacked = jnp.concatenate([student, teacher_scaled], axis=0)
    local_peak = jnp.max(stacked, axis=2)
    highest = lax.pmax(local_peak, "vocab")
    summed = lax.psum(jnp.sum(jnp.exp(stacked - highest[:, :, None]), axis=2), "vocab")
    softmaxes = jnp.exp(stacked - highest[:, :, None]) / summed[:, :, None]
    offset = lax.axis_index("vocab") * block_width
    columns = jnp.arange(block_width, dtype=jnp.int32)[None, :] + offset
    onehot = (columns == labels[:, None]).astype(jnp.float32)
    heat_count = temps.shape[0]
    logit_grad = mix[0] * (softmaxes[0] - onehot)
    weights = mix[1] * temps
    logit_grad = logit_grad + jnp.einsum(
        "k,kab->ab", weights, softmaxes[1 : 1 + heat_count] - softmaxes[1 + heat_count :]
    )
    logit_grad = logit_grad.astype(jnp.bfloat16)
    grad_all = lax.all_gather(logit_grad, "dp", axis=0, tiled=True)
    head_grad = jnp.dot(h_block, grad_all, preferred_element_type=jnp.float32).astype(jnp.bfloat16)
    hidden_grad = lax.psum_scatter(
        lax.dot_general(
            head, grad_all, (((1,), (1,)), ((), ())), preferred_element_type=jnp.float32
        ),
        "vocab",
        scatter_dimension=0,
        tiled=True,
    )
    return (hidden_grad, head_grad)


def solution(mesh):
    placed = (P(("dp", "vocab"), None), P("dp", "vocab"), P("dp", "vocab"), P("dp"), P(), P())
    return jax.shard_map(
        shards,
        mesh=mesh,
        in_specs=placed,
        out_specs=(P(("dp", "vocab"), None), P("dp", "vocab")),
        check_vma=False,
    )
```

profile of v0, /device:TPU:6, one launch (start us, length us, event | category | flops | bytes accessed | tf_op | source)
XLA Modules:
  0.0 861.4 jit_solution(14187076467342216205)
XLA Ops:
  7.2 0.7 all-gather.3.cloned.1.call-update
  8.0 83.7 %all-gather.3.cloned.1.call-done = bf16[2048,768]{1,0:T(8,128)(2,1)} async-done(((bf16[32,768]{1,0:T(8,128)(2,1)}), bf16[2048,768]{1,0:T(8,128)(2,1)}) %all-gather.3.cloned.1.call-update) | async-done | bytes 3145744 | tf_op jit(solution)/shard_map/all_gather | solution.py:8
  91.7 9.7 %fusion.14 = f32[768,1280]{1,0:T(8,128)} fusion(bf16[2048,768]{1,0:T(8,128)(2,1)} %all-gather.3.cloned.1.call-done, bf16[2048,1280]{1,0:T(8,128)(2,1)} %param.7), kind=kOutput, calls=%fused_computation.24 | convolution fusion | flops 4026531840 | bytes 12320768 | tf_op jit(solution)/shard_map/dot_general | solution.py:11
  101.5 0.5 copy-done.4
  102.0 0.6 fusion.13
  102.7 41.7 %reduce-scatter.5.cloned.1.call-done = f32[192,1280]{1,0:T(8,128)} async-done(((f32[768,1280]{1,0:T(8,128)}), f32[192,1280]{1,0:T(8,128)}) %reduce-scatter.5.cloned.1.call-update) | async-done | bytes 983056 | tf_op jit(solution)/shard_map/reduce_scatter | solution.py:10
  144.3 2.0 broadcast_multiply_fusion.1
  146.4 1.8 copy-done
  148.2 1.4 copy-done.1
  149.6 0.8 fusion.5
  150.4 251.0 %pmax.7 = f32[9,192]{1,0:T(8,128)S(1)} all-reduce(f32[9,192]{1,0:T(8,128)S(1)} %fusion.5), channel_id=1, replica_groups=mesh['dp'=4,'vocab'=64] {'vocab'}, use_global_device_ids=true, to_apply=%region_2.0 | all-reduce | flops 1728 | bytes 13824 | tf_op jit(solution)/shard_map/pmax | solution.py:24
  401.4 4.3 fusion.1
  405.7 246.1 %psum.7 = f32[9,192]{1,0:T(8,128)S(1)} all-reduce(f32[9,192]{1,0:T(8,128)S(1)} %fusion.1), channel_id=1, replica_groups=mesh['dp'=4,'vocab'=64] {'vocab'}, use_global_device_ids=true, to_apply=%region_4.0 | all-reduce | flops 1728 | bytes 13824 | tf_op jit(solution)/shard_map/psum | solution.py:25
  651.8 4.6 fusion
  656.4 0.5 slice_subtract_fusion
  656.9 2.2 fusion.3
  659.2 1.7 fusion.9
  661.1 26.7 %all-gather.5.cloned.1.call-done = bf16[768,1280]{1,0:T(8,128)(2,1)} async-done(((bf16[192,1280]{1,0:T(8,128)(2,1)}), bf16[768,1280]{1,0:T(8,128)(2,1)}) %all-gather.5.cloned.1.call-update) | async-done | bytes 1966096 | tf_op jit(solution)/shard_map/all_gather | solution.py:37
  687.8 10.0 %convolution_bitcast_fusion = f32[2048,768]{0,1:T(8,128)} fusion(bf16[768,1280]{1,0:T(8,128)(2,1)} %all-gather.5.cloned.1.call-done, bf16[2048,1280]{1,0:T(8,128)(2,1)} %param.7), kind=kOutput, calls=%fused_computation.9 | convolution fusion | flops 4026531840 | bytes 13500416 | tf_op jit(solution)/shard_map/dot_general | solution.py:40
  697.8 6.6 copy.16
  704.4 1.9 copy-done.6
  706.3 7.6 fusion.2
  713.9 7.9 copy.13
  721.7 133.1 %reduce-scatter.7.cloned.1.call-done = f32[32,768]{1,0:T(8,128)} async-done(((f32[2048,768]{1,0:T(8,128)}), f32[32,768]{1,0:T(8,128)}) %reduce-scatter.7.cloned.1.call-update) | async-done | bytes 98320
  (22 shorter events, 0.5 us)
Async XLA Ops:
  7.2 84.5 %all-gather.3.cloned.1.call-start = ((), (), s32[]{:S(2)}) async-start(), calls=%async_computation.2 | async-start | bytes 3194880 | tf_op jit(solution)/shard_map/all_gather | solution.py:8
  7.9 93.5 %copy-start.3 = (bf16[192,1280]{1,0:T(8,128)(2,1)S(1)}, bf16[192,1280]{1,0:T(8,128)(2,1)}, u32[]{:S(2)}) copy-start(bf16[192,1280]{1,0:T(8,128)(2,1)} %param.8) | copy-start | bytes 1474564
  7.9 136.4 %reduce-scatter.5.cloned.1.call-start = ((), (), s32[]{:S(2)}) async-start(), calls=%async_computation.3 | async-start | bytes 4915200 | tf_op jit(solution)/shard_map/reduce_scatter | solution.py:10
  101.3 0.7 copy-start.4
  101.3 1.3 copy-start.7
  101.4 586.5 %all-gather.5.cloned.1.call-start = ((), (), s32[]{:S(2)}) async-start(), calls=%async_computation.4 | async-start | bytes 2457600 | tf_op jit(solution)/shard_map/all_gather | solution.py:37
  144.3 5.3 copy-start.2
  146.4 1.9 copy-start
  146.4 3.2 copy-start.1
  656.4 2.7 copy-start.5
  660.9 194.0 %reduce-scatter.7.cloned.1.call-start = ((), (), s32[]{:S(2)}) async-start(), calls=%async_computation.5 | async-start | bytes 6389760
  704.4 1.9 copy-start.6
Sparse Core Ops, SparseCore 0:
  10.7 80.8 all-gather.2
  101.5 42.7 reduce-scatter.4
  661.0 26.8 all-gather.4
  704.5 150.3 reduce-scatter.6
where the time goes:
time: 862 us; the launch traced here: 861 us
  blocking collectives  497 us (58%)
  waiting for transfers between devices  286 us (33%)
  matrix products  29.5 us (3%)
  local copies, waits for them, and re-layouts  20.7 us (2%)
  other arithmetic  13.9 us (2%)
  between operations  13.9 us (2%)
    pmax x1, blocking collectives, shards(): highest = lax.pmax(local_peak, 'vocab')  251 us
    psum x1, blocking collectives, shards(): lax.psum(jnp.sum(jnp.exp(stacked - highest[:, :, None]), axis=2), 'vocab')  246 us
    unnamed x5, waiting for transfers between devices  134 us
    all_gather x1, waiting for transfers between devices, shards(): h_block = lax.all_gather(hidden_t, 'vocab', axis=0, tiled=True)  83.7 us
    reduce_scatter x1, waiting for transfers between devices, shards(): lax.psum_scatter(lax.dot_general(h_block, head, (((0,), (0,)), ((), ())),...  41.7 us
    all_gather x1, waiting for transfers between devices, shards(): grad_all = lax.all_gather(logit_grad, 'dp', axis=0, tiled=True)  26.7 us
    unnamed x18, local copies, waits for them, and re-layouts  20 us
  transfers between devices with their start and end apart: 4, of which 4 were waited for; matrix products, arithmetic and copies ran while one was open for 2% of the time, Pallas kernels for 0%

commit v1 on v0

--- a/solution.py
+++ b/solution.py
@@ -22,7 +22,9 @@
     stacked = jnp.concatenate([student, teacher_scaled], axis=0)
     local_peak = jnp.max(stacked, axis=2)
     highest = lax.pmax(local_peak, "vocab")
-    summed = lax.psum(jnp.sum(jnp.exp(stacked - highest[:, :, None]), axis=2), "vocab")
+    summed = jnp.sum(
+        lax.all_gather(jnp.sum(jnp.exp(stacked - highest[:, :, None]), axis=2), "vocab"), axis=0
+    )
     softmaxes = jnp.exp(stacked - highest[:, :, None]) / summed[:, :, None]
     offset = lax.axis_index("vocab") * block_width
     columns = jnp.arange(block_width, dtype=jnp.int32)[None, :] + offset

time: 862 us -> 666 us (0.77)
  blocking collectives: 497 us -> 298 us
    psum x1 -> x0, blocking collectives: 246 us -> none  [shards(): lax.psum(jnp.sum(jnp.exp(stacked - highest[:, :, None]), axis=2), 'vocab')]
    all_gather x0 -> x1, blocking collectives: none -> 47.4 us  [shards(): lax.all_gather(jnp.sum(jnp.exp(stacked - highest[:, :, None]), axis=2), '...]
where the time goes in v1:
time: 666 us; the launch traced here: 665 us
  blocking collectives  298 us (45%)
  waiting for transfers between devices  289 us (43%)
  matrix products  29.5 us (4%)
  local copies, waits for them, and re-layouts  20.7 us (3%)
  other arithmetic  14.1 us (2%)
  between operations  13.9 us (2%)
    pmax x1, blocking collectives, shards(): highest = lax.pmax(local_peak, 'vocab')  251 us
    unnamed x5, waiting for transfers between devices  134 us
    all_gather x1, waiting for transfers between devices, shards(): h_block = lax.all_gather(hidden_t, 'vocab', axis=0, tiled=True)  83.7 us
    all_gather x1, blocking collectives, shards(): lax.all_gather(jnp.sum(jnp.exp(stacked - highest[:, :, None]), axis=2), '...  47.4 us
    reduce_scatter x1, waiting for transfers between devices, shards(): lax.psum_scatter(lax.dot_general(h_block, head, (((0,), (0,)), ((), ())),...  41.7 us
    all_gather x1, waiting for transfers between devices, shards(): grad_all = lax.all_gather(logit_grad, 'dp', axis=0, tiled=True)  29.5 us
    unnamed x18, local copies, waits for them, and re-layouts  20 us
  transfers between devices with their start and end apart: 4, of which 4 were waited for; matrix products, arithmetic and copies ran while one was open for 2% of the time, Pallas kernels for 0%

profile of v1, /device:TPU:6, one launch (start us, length us, event | category | flops | bytes accessed | tf_op | source)
XLA Modules:
  0.0 665.2 jit_solution(7882367480892810833)
XLA Ops:
  7.2 0.7 all-gather.5.cloned.1.call-update
  8.0 83.7 %all-gather.5.cloned.1.call-done = bf16[2048,768]{1,0:T(8,128)(2,1)} async-done(((bf16[32,768]{1,0:T(8,128)(2,1)}), bf16[2048,768]{1,0:T(8,128)(2,1)}) %all-gather.5.cloned.1.call-update) | async-done | bytes 3145744 | tf_op jit(solution)/shard_map/all_gather | solution.py:8
  91.7 9.7 %fusion.14 = f32[768,1280]{1,0:T(8,128)} fusion(bf16[2048,768]{1,0:T(8,128)(2,1)} %all-gather.5.cloned.1.call-done, bf16[2048,1280]{1,0:T(8,128)(2,1)} %param.7), kind=kOutput, calls=%fused_computation.24 | convolution fusion | flops 4026531840 | bytes 12320768 | tf_op jit(solution)/shard_map/dot_general | solution.py:11
  101.5 0.5 copy-done.4
  102.0 0.6 fusion.13
  102.7 41.7 %reduce-scatter.5.cloned.1.call-done = f32[192,1280]{1,0:T(8,128)} async-done(((f32[768,1280]{1,0:T(8,128)}), f32[192,1280]{1,0:T(8,128)}) %reduce-scatter.5.cloned.1.call-update) | async-done | bytes 983056 | tf_op jit(solution)/shard_map/reduce_scatter | solution.py:10
  144.3 2.0 broadcast_multiply_fusion.1
  146.4 1.8 copy-done
  148.2 1.4 copy-done.1
  149.6 0.8 fusion.5
  150.4 251.0 %pmax.7 = f32[9,192]{1,0:T(8,128)S(1)} all-reduce(f32[9,192]{1,0:T(8,128)S(1)} %fusion.5), channel_id=1, replica_groups=mesh['dp'=4,'vocab'=64] {'vocab'}, use_global_device_ids=true, to_apply=%region_2.0 | all-reduce | flops 1728 | bytes 13824 | tf_op jit(solution)/shard_map/pmax | solution.py:24
  401.4 4.3 fusion.1
  405.7 47.4 %all-gather.1 = f32[64,9,192]{2,1,0:T(8,128)S(1)} all-gather(f32[1,9,192]{2,1,0:T(8,128)S(1)} %bitcast.33), channel_id=2, replica_groups=mesh['dp'=4,'vocab'=64] {'vocab'}, dimensions={0}, use_global_device_ids=true | all-gather | bytes 449280 | tf_op jit(solution)/shard_map/all_gather | solution.py:26
  453.2 4.6 fusion
  457.8 0.5 slice_subtract_fusion
  458.3 2.2 fusion.3
  460.5 1.7 fusion.9
  462.3 29.5 %all-gather.7.cloned.1.call-done = bf16[768,1280]{1,0:T(8,128)(2,1)} async-done(((bf16[192,1280]{1,0:T(8,128)(2,1)}), bf16[768,1280]{1,0:T(8,128)(2,1)}) %all-gather.7.cloned.1.call-update) | async-done | bytes 1966096 | tf_op jit(solution)/shard_map/all_gather | solution.py:39
  491.8 10.0 %convolution_bitcast_fusion = f32[2048,768]{0,1:T(8,128)} fusion(bf16[768,1280]{1,0:T(8,128)(2,1)} %all-gather.7.cloned.1.call-done, bf16[2048,1280]{1,0:T(8,128)(2,1)} %param.7), kind=kOutput, calls=%fused_computation.9 | convolution fusion | flops 4026531840 | bytes 13500416 | tf_op jit(solution)/shard_map/dot_general | solution.py:42
  501.8 6.6 copy.16
  508.4 1.9 copy-done.6
  510.2 7.6 %fusion.2 = bf16[2048,1280]{0,1:T(8,128)(2,1)} fusion(bf16[768,1280]{1,0:T(8,128)(2,1)} %all-gather.7.cloned.1.call-done, bf16[2048,768]{1,0:T(8,128)(2,1)S(1)} %copy-done.6), kind=kOutput, calls=%fused_computation.5 | convolution fusion | flops 4029153280 | bytes 10354688 | tf_op jit(solution)/shard_map/dot_general | solution.py:40
  517.8 7.9 %copy.13 = bf16[2048,1280]{1,0:T(8,128)(2,1)} copy(bf16[2048,1280]{0,1:T(8,128)(2,1)} %fusion.2) | data formatting | bytes 10485760
  525.7 132.9 %reduce-scatter.7.cloned.1.call-done = f32[32,768]{1,0:T(8,128)} async-done(((f32[2048,768]{1,0:T(8,128)}), f32[32,768]{1,0:T(8,128)}) %reduce-scatter.7.cloned.1.call-update) | async-done | bytes 98320
  (23 shorter events, 0.4 us)
Async XLA Ops:
  7.2 84.5 %all-gather.5.cloned.1.call-start = ((), (), s32[]{:S(2)}) async-start(), calls=%async_computation.2 | async-start | bytes 3194880 | tf_op jit(solution)/shard_map/all_gather | solution.py:8
  7.9 93.5 %copy-start.3 = (bf16[192,1280]{1,0:T(8,128)(2,1)S(1)}, bf16[192,1280]{1,0:T(8,128)(2,1)}, u32[]{:S(2)}) copy-start(bf16[192,1280]{1,0:T(8,128)(2,1)} %param.8) | copy-start | bytes 1474564
  7.9 136.4 %reduce-scatter.5.cloned.1.call-start = ((), (), s32[]{:S(2)}) async-start(), calls=%async_computation.3 | async-start | bytes 4915200 | tf_op jit(solution)/shard_map/reduce_scatter | solution.py:10
  101.3 0.7 copy-start.4
  101.3 1.3 copy-start.7
  101.4 390.4 %all-gather.7.cloned.1.call-start = ((), (), s32[]{:S(2)}) async-start(), calls=%async_computation.4 | async-start | bytes 2457600 | tf_op jit(solution)/shard_map/all_gather | solution.py:39
  144.3 5.3 copy-start.2
  146.4 1.9 copy-start
  146.4 3.2 copy-start.1
  457.8 2.7 copy-start.5
  462.2 196.4 %reduce-scatter.7.cloned.1.call-start = ((), (), s32[]{:S(2)}) async-start(), calls=%async_computation.5 | async-start | bytes 6389760
  508.3 1.9 copy-start.6
Sparse Core Ops, SparseCore 0:
  10.7 80.8 all-gather.4
  101.5 42.7 reduce-scatter.4
  462.4 29.3 all-gather.6
  508.5 150.0 reduce-scatter.6
